TPU v7x, 32 devices: a whole 2x2x4 slice. The times are simulated.
32 devices in a mesh: groups: 2 (over x), tile: 16 (over z, y, core).
Axes of the slice: x: 2, y: 2, z: 4, core: 2. Of those that a mesh axis runs over, the one named last changes fastest.
Arguments:
- latent_rows: bfloat16 [4096, 256], P(('groups', 'tile')), parts along dimension 0, may hold values from -6 to 6
- line_order: int32 [128], P('groups'), parts along dimension 0, may hold values from 0 to 63, each once
- conv_weight: bfloat16 [3, 3, 3, 256, 128], replicated, may hold values from -0.078125 to 0.078125
- conv_bias: float32 [128], replicated, may hold values from -3 to 3
- blend_table: float32 [4, 8], replicated, may hold values from 0.25 to 4
- blend_ids: int32 [32], P('groups'), parts along dimension 0, may hold values from 0 to 3
Outputs:
- frames: bfloat16 [16, 32, 64, 128], P('groups', None, 'tile'), parts along dimension 0
There are 2 independent parts, one for each index of `groups`. A program takes and returns all parts, laid end to end along the dimension named above; an argument that names none is the same for every part. Nothing has to cross between parts.
Inputs may be any that keep to these rules, and one draw needn't show every extreme that they name: line_order is a permutation of the 64 latent lines.
All inputs are finite; a program needn't handle non-finite values.
Results may differ from a plain program's by a relative error of at most 0.001.
Values may be sent and summed in bfloat16 or wider, within the bound.
A program may use at most 64 MiB of HBM per device.

v0:
```python
import jax
import jax.numpy as jnp
from jax import lax
from jax.sharding import PartitionSpec as P

LT = 4
WD = 2


def from_behind(value, axis, steps):
    count = lax.axis_size(axis)
    initial, last = (max(0, -steps), min(count, count - steps))
    return lax.ppermute(value, axis, [(source, source + steps) for source in range(initial, last)])


def upsample(values):
    values = jnp.repeat(values, 2, axis=0)
    values = jnp.repeat(values, 2, axis=1)
    return jnp.repeat(values, 2, axis=2)


def decode_tile(window, conv_weight, conv_bias):
    upsampled = upsample(window)
    upsampled = jnp.concatenate([upsampled[:1], upsampled[:1], upsampled], axis=0)
    output = lax.conv_general_dilated(
        upsampled[None],
        conv_weight,
        (1, 1, 1),
        [(0, 0), (1, 1), (1, 1)],
        dimension_numbers=("NDHWC", "DHWIO", "NDHWC"),
        preferred_element_type=jnp.float32,
    )[0]
    return jax.nn.silu(output + conv_bias)


def blend_profile(blend_table, blend_ids, tile_at):
    kind_index = lax.dynamic_index_in_dim(blend_ids, tile_at, 0, keepdims=False)
    selector = (jnp.arange(blend_table.shape[0], dtype=jnp.int32) == kind_index).astype(jnp.float32)
    return jnp.sum(selector[:, None] * blend_table, axis=0)


def per_device(latent_rows, line_order, conv_weight, conv_bias, blend_table, blend_ids):
    tile_count = lax.axis_size("tile")
    position = lax.axis_index("tile")
    channels = latent_rows.shape[1]
    lines_dev = latent_rows.shape[0] // (WD * tile_count)
    blocks = latent_rows.reshape(lines_dev, tile_count, WD, channels)
    zero_col = jnp.zeros((lines_dev, 1, 1, channels), latent_rows.dtype)
    lower_cols = jnp.concatenate([zero_col, blocks[:, :-1, -1:]], axis=1)
    upper_cols = jnp.concatenate([blocks[:, 1:, :1], zero_col], axis=1)
    widened = jnp.concatenate([lower_cols, blocks, upper_cols], axis=2)
    received = lax.all_to_all(widened, "tile", split_axis=1, concat_axis=0, tiled=True)
    width_now = WD + 2
    line_count = received.shape[0]
    gathered_rows = received.reshape(line_count, width_now, channels)
    inverse = (
        jnp.zeros((line_count,), jnp.int32)
        .at[line_order]
        .set(jnp.arange(line_count, dtype=jnp.int32))
    )
    latent = gathered_rows[inverse].reshape(LT, line_count // LT, width_now, channels)
    decoded = decode_tile(latent, conv_weight, conv_bias)
    lower_at = jnp.maximum(position - 1, 0)
    upper_at = jnp.minimum(position + 1, tile_count - 1)
    has_lower = (position > 0).astype(jnp.float32)
    has_upper = (position < tile_count - 1).astype(jnp.float32)
    weight_self = blend_profile(blend_table, blend_ids, position)
    weight_lower = blend_profile(blend_table, blend_ids, lower_at)
    weight_upper = blend_profile(blend_table, blend_ids, upper_at)
    weighted = decoded * weight_self[None, None, :, None]
    from_lower = from_behind(weighted[:, :, -2:], "tile", 1)
    from_upper = from_behind(weighted[:, :, :2], "tile", -1)
    blended = weighted[:, :, 2:-2]
    blended = blended.at[:, :, :2].add(from_lower)
    blended = blended.at[:, :, -2:].add(from_upper)
    weight_sum = weight_self[2:-2]
    weight_sum = weight_sum.at[:2].add(has_lower * weight_lower[-2:])
    weight_sum = weight_sum.at[-2:].add(has_upper * weight_upper[:2])
    return (blended / weight_sum[None, None, :, None]).astype(jnp.bfloat16)


def solution(mesh):
    return jax.shard_map(
        per_device,
        mesh=mesh,
        in_specs=(P(("groups", "tile"), None), P("groups"), P(), P(), P(), P("groups")),
        out_specs=P("groups", None, "tile", None),
        check_vma=False,
    )
```

profile of v0, /device:TPU:1, one launch (start us, length us, event | category | flops | bytes accessed | tf_op | source)
XLA Modules:
  0.0 53.6 jit_solution(13139769069828558887)
XLA Ops:
  0.0 0.0 copy-start
  0.0 1.0 %reshape.160 = bf16[4,16,2,256]{3,2,1,0:T(2,128)(2,1)S(1)} reshape(bf16[128,256]{1,0:T(8,128)(2,1)} %param.14) | data formatting | bytes 131072 | tf_op jit(solution)/shard_map/reshape | solution.py:47
  1.0 0.1 fusion.11
  1.1 0.9 %fusion.6 = bf16[4,16,4,256]{3,2,0,1:T(4,128)(2,1)} fusion(bf16[4,15,1,256]{3,2,0,1:T(2,128)(2,1)S(1)} %get-tuple-element.59, bf16[4,15,1,256]{3,2,0,1:T(2,128)(2,1)S(1)} %get-tuple-element.58, bf16[4,16,2,256]{3,2,1,0:T(2,128)(2,1)S(1)} %reshape.160), kind=kLoop, calls=%fused_computation.15 | loop fusion | flops 655360 | bytes 258048 | tf_op jit(solution)/shard_map/concatenate | solution.py:51
  2.0 7.3 %all-to-all-start = ((bf16[4,16,4,256]{3,2,0,1:T(4,128)(2,1)}), bf16[4,16,4,256]{3,2,0,1:T(4,128)(2,1)S(1)}, u32[]{:S(2)}, u32[]{:S(2)}) async-start(bf16[4,16,4,256]{3,2,0,1:T(4,128)(2,1)} %fusion.6), calls=%async_computation | async-start | bytes 262144 | tf_op jit(solution)/shard_map/all_to_all | solution.py:52
  9.4 1.4 %fusion.12 = (s32[1]{0:T(128)}, s32[1]{0:T(128)}, s32[1]{0:T(128)}) fusion(s32[16]{0:T(128)} %param.19, s32[]{:T(128)S(6)} %max.3, s32[]{:T(128)S(6)} %select_n.16, s32[]{:T(128)S(6)} %select_n.17), kind=kLoop, calls=%fused_computation.33 | loop fusion | bytes 36 | tf_op jit(solution)/shard_map/jit(dynamic_index_in_dim)/dynamic_slice | solution.py:37
  10.8 0.6 %compare_convert_fusion.2 = f32[4]{0:T(128)S(1)} fusion(s32[]{:T(128)} %bitcast.10), kind=kLoop, calls=%fused_computation.26 | loop fusion | flops 8 | bytes 20 | tf_op jit(solution)/shard_map/convert_element_type | solution.py:38
  11.4 1.2 %compare_convert_fusion = (f32[4]{0:T(128)S(1)}, f32[4]{0:T(128)S(1)}) fusion(s32[]{:T(128)} %bitcast.12, s32[]{:T(128)} %bitcast.11), kind=kLoop, calls=%fused_computation.24 | loop fusion | flops 16 | bytes 40 | tf_op jit(solution)/shard_map/convert_element_type | solution.py:38
  12.6 0.8 %multiply_reduce_fusion = (f32[8]{0:T(128)S(1)}, f32[8]{0:T(128)S(1)}, f32[8]{0:T(128)S(1)}) fusion(f32[4,8]{1,0:T(4,128)} %param.18, f32[4]{0:T(128)S(1)} %get-tuple-element.63, f32[4]{0:T(128)S(1)} %compare_convert_fusion.2, f32[4]{0:T(128)S(1)} %get-tuple-element.64), kind=kLoop, calls=%fused_computation.21 | loop fusion | flops 168 | bytes 272 | tf_op jit(solution)/shard_map/reduce_sum | solution.py:39
  13.4 0.1 slice.131
  13.5 0.7 %compare_select_fusion.1 = s32[64]{0:T(128)S(1)} fusion(s32[64]{0:T(128)} %param.15), kind=kLoop, calls=%fused_computation.20 | loop fusion | flops 192 | bytes 512 | tf_op jit(solution)/shard_map/select_n | solution.py:59
  14.1 0.8 %scatter_custom_fusion = s32[64]{0:T(128)S(1)} fusion(s32[64]{0:T(128)S(1)} %compare_select_fusion.1, s32[64]{0:T(128)S(1)} %iota.18, s32[]{:T(128)} %constant.121.clone.1), kind=kCustom, calls=%fused_computation.29 | custom fusion | bytes 260 | tf_op jit(solution)/shard_map/scatter | solution.py:59
  14.9 1.2 %all-to-all-done = bf16[4,16,4,256]{3,2,0,1:T(4,128)(2,1)S(1)} async-done(((bf16[4,16,4,256]{3,2,0,1:T(4,128)(2,1)}), bf16[4,16,4,256]{3,2,0,1:T(4,128)(2,1)S(1)}, u32[]{:S(2)}, u32[]{:S(2)}) %all-to-all-start) | async-done | bytes 131104 | tf_op jit(solution)/shard_map/all_to_all | solution.py:52
  16.1 0.7 %gather_fusion = bf16[64,4,256]{2,1,0:T(4,128)(2,1)S(1)} fusion(bf16[64,4,256]{2,1,0:T(4,128)(2,1)S(1)} %bitcast.24, s32[1024]{0:T(1024)S(1)} %pad_clamp_fusion), kind=kCustom, calls=%fused_computation | custom fusion | bytes 262400 | tf_op jit(solution)/shard_map/gather | solution.py:61
  16.8 0.1 broadcast_in_dim.35
  17.0 0.1 broadcast_in_dim.38
  17.0 0.1 broadcast_in_dim.39
  17.1 0.1 broadcast_in_dim.40
  17.3 1.7 %broadcast_in_dim.41 = bf16[8,32,4,2,256]{4,3,2,1,0:T(2,128)(2,1)} broadcast(bf16[8,32,4,256]{3,2,1,0:T(4,128)(2,1)S(1)} %bitcast.19), dimensions={0,1,2,4} | broadcast | bytes 1572864 | tf_op jit(solution)/shard_map/broadcast_in_dim | solution.py:19
  19.0 1.5 %reshape.165 = bf16[8,32,8,256]{3,2,1,0:T(8,128)(2,1)S(1)} reshape(bf16[8,32,4,2,256]{4,3,2,1,0:T(2,128)(2,1)} %broadcast_in_dim.41) | data formatting | bytes 2097152 | tf_op jit(solution)/shard_map/reshape | solution.py:19
  20.4 0.1 maximum_bitcast_fusion
  20.5 0.0 copy-done
  20.6 0.0 copy-start.1
  20.6 20.3 %fusion = f32[1,8,32,8,128]{4,0,3,2,1:T(1,128)S(1)} fusion(bf16[3,3,3,256,128]{4,3,2,1,0:T(8,128)(2,1)S(1)} %copy-done, bf16[1,10,32,8,256]{4,3,2,1,0:T(8,128)(2,1)S(1)} %maximum_bitcast_fusion), kind=kOutput, calls=%fused_computation.2 | convolution fusion | flops 3252682752 | bytes 4128768 | tf_op jit(solution)/shard_map/conv_general_dilated | solution.py:25
  40.9 0.0 copy-done.1
  40.9 0.3 multiply_multiply_fusion
  41.2 0.9 %fusion.10 = (f32[8,32,2,128]{3,2,1,0:T(2,128)S(1)}, f32[8,32,2,128]{3,2,1,0:T(2,128)}) fusion(f32[8,32,8,128]{3,2,1,0:T(8,128)S(1)} %multiply_multiply_fusion), kind=kLoop, calls=%fused_computation.31 | loop fusion | bytes 1048576 | tf_op jit(solution)/shard_map/slice | solution.py:72
  42.1 2.3 %collective-permute-start = (f32[8,32,2,128]{3,2,1,0:T(2,128)}, f32[8,32,2,128]{3,2,1,0:T(2,128)S(1)}, u32[]{:S(2)}, u32[]{:S(2)}) collective-permute-start(f32[8,32,2,128]{3,2,1,0:T(2,128)} %get-tuple-element.57), channel_id=1, source_target_pairs={{0,1},{1,2},{2,3},{3,4},{4,5},{5,6},{6,7},{7,8},{8,9},{9,10},{10,1... | collective-permute-start | bytes 786440 | tf_op jit(solution)/shard_map/ppermute | solution.py:13
  44.4 0.1 constant_dynamic-update-slice_fusion.1
  44.5 0.2 constant_dynamic-update-slice_fusion
  44.6 0.1 slice.141
  44.8 2.1 %collective-permute-start.1 = (f32[8,32,2,128]{3,2,1,0:T(2,128)S(1)}, f32[8,32,2,128]{3,2,1,0:T(2,128)S(1)}, u32[]{:S(2)}, u32[]{:S(2)}) collective-permute-start(f32[8,32,2,128]{3,2,1,0:T(2,128)S(1)} %get-tuple-element.56), channel_id=1, source_target_pairs={{1,0},{2,1},{3,2},{4,3},{5,4},{6,5},{7,6},{8,7},{9,8},{10,9},{11,1... | collective-permute-start | bytes 786440 | tf_op jit(solution)/shard_map/ppermute | solution.py:13
  46.9 1.1 %collective-permute-done = f32[8,32,2,128]{3,2,1,0:T(2,128)S(1)} collective-permute-done((f32[8,32,2,128]{3,2,1,0:T(2,128)}, f32[8,32,2,128]{3,2,1,0:T(2,128)S(1)}, u32[]{:S(2)}, u32[]{:S(2)}) %collective-permute-start) | collective-permute-done | bytes 262176 | tf_op jit(solution)/shard_map/ppermute | solution.py:13
  48.0 0.2 fusion.3
  48.3 4.2 %collective-permute-done.1 = f32[8,32,2,128]{3,2,1,0:T(2,128)S(1)} collective-permute-done((f32[8,32,2,128]{3,2,1,0:T(2,128)S(1)}, f32[8,32,2,128]{3,2,1,0:T(2,128)S(1)}, u32[]{:S(2)}, u32[]{:S(2)}) %collective-permute-start.1) | collective-permute-done | bytes 262176 | tf_op jit(solution)/shard_map/ppermute | solution.py:13
  52.5 0.3 fusion.2
  52.7 0.9 %divide_convert_fusion = bf16[8,32,4,128]{3,2,1,0:T(4,128)(2,1)} fusion(f32[8,32,4,128]{3,2,1,0:T(4,128)S(1)} %fusion.2, f32[4]{0:T(128)S(1)} %constant_dynamic-update-slice_fusion), kind=kLoop, calls=%fused_computation.6 | loop fusion | flops 262144 | bytes 786448 | tf_op jit(solution)/shard_map/convert_element_type | solution.py:79
  (5 shorter events, 0.0 us)
Async XLA Ops:
  0.0 20.5 %copy-start = (bf16[3,3,3,256,128]{4,3,2,1,0:T(8,128)(2,1)S(1)}, bf16[3,3,3,256,128]{4,3,2,1,0:T(8,128)(2,1)}, u32[]{:S(2)}) copy-start(bf16[3,3,3,256,128]{4,3,2,1,0:T(8,128)(2,1)} %param.16) | copy-start | bytes 5308420
  2.0 14.1 %all-to-all-start = ((bf16[4,16,4,256]{3,2,0,1:T(4,128)(2,1)}), bf16[4,16,4,256]{3,2,0,1:T(4,128)(2,1)S(1)}, u32[]{:S(2)}, u32[]{:S(2)}) async-start(bf16[4,16,4,256]{3,2,0,1:T(4,128)(2,1)} %fusion.6), calls=%async_computation | async-start | bytes 262144 | tf_op jit(solution)/shard_map/all_to_all | solution.py:52
  20.6 20.3 %copy-start.1 = (f32[128]{0:T(128)S(1)}, f32[128]{0:T(128)}, u32[]{:S(2)}) copy-start(f32[128]{0:T(128)} %param.17) | copy-start | bytes 1540
  42.1 5.9 %collective-permute-start = (f32[8,32,2,128]{3,2,1,0:T(2,128)}, f32[8,32,2,128]{3,2,1,0:T(2,128)S(1)}, u32[]{:S(2)}, u32[]{:S(2)}) collective-permute-start(f32[8,32,2,128]{3,2,1,0:T(2,128)} %get-tuple-element.57), channel_id=1, source_target_pairs={{0,1},{1,2},{2,3},{3,4},{4,5},{5,6},{6,7},{7,8},{8,9},{9,10},{10,1... | collective-permute-start | bytes 786440 | tf_op jit(solution)/shard_map/ppermute | solution.py:13
  44.8 7.7 %collective-permute-start.1 = (f32[8,32,2,128]{3,2,1,0:T(2,128)S(1)}, f32[8,32,2,128]{3,2,1,0:T(2,128)S(1)}, u32[]{:S(2)}, u32[]{:S(2)}) collective-permute-start(f32[8,32,2,128]{3,2,1,0:T(2,128)S(1)} %get-tuple-element.56), channel_id=1, source_target_pairs={{1,0},{2,1},{3,2},{4,3},{5,4},{6,5},{7,6},{8,7},{9,8},{10,9},{11,1... | collective-permute-start | bytes 786440 | tf_op jit(solution)/shard_map/ppermute | solution.py:13
where the time goes:
time: 54 us; the launch traced here: 53.6 us
  matrix products  20.3 us (38%)
  starting transfers between devices  11.8 us (22%)
  local copies, waits for them, and re-layouts  8.63 us (16%)
  waiting for transfers between devices  6.55 us (12%)
  other arithmetic  6.2 us (11%)
    conv_general_dilated x1, matrix products, decode_tile(): lax.conv_general_dilated(upsampled[None], conv_weight, (1, 1, 1), [(0, 0)...  20.3 us
    all_to_all x1, starting transfers between devices, per_device(): lax.all_to_all(widened, 'tile', split_axis=1, concat_axis=0, tiled=True)  7.34 us
    ppermute x2, waiting for transfers between devices, from_behind(): lax.ppermute(value, axis, [(source, source + steps) for source in range(i...  5.34 us
    ppermute x2, starting transfers between devices, from_behind(): lax.ppermute(value, axis, [(source, source + steps) for source in range(i...  4.42 us
    broadcast_in_dim x3, local copies, waits for them, and re-layouts, upsample(): return jnp.repeat(values, 2, axis=2)  1.84 us
    convert_element_type x2, other arithmetic, blend_profile(): (jnp.arange(blend_table.shape[0], dtype=jnp.int32) == kind_index).astype(...  1.83 us
    reshape x1, local copies, waits for them, and re-layouts, upsample(): return jnp.repeat(values, 2, axis=2)  1.47 us
    dynamic_slice x1, local copies, waits for them, and re-layouts, blend_profile(): kind_index = lax.dynamic_index_in_dim(blend_ids, tile_at, 0, keepdims=False)  1.42 us
  transfers between devices with their start and end apart: 3, of which 3 were waited for; matrix products, arithmetic and copies ran while one was open for 11% of the time, Pallas kernels for 0%

commit v1 on v0

v1 whole, which is shorter than its diff:
```python
import functools

import jax
import jax.numpy as jnp
from jax import lax
from jax.experimental import pallas as pl
from jax.experimental.pallas import tpu as pltpu
from jax.sharding import PartitionSpec as P

LT = 4
WD = 2
KW = WD + 2
F32 = jnp.float32
BF16 = jnp.bfloat16
MESH = pl.DeviceIdType.MESH


def log2(n):
    assert n & (n - 1) == 0
    return n.bit_length() - 1


def iota(shape, dim):
    return lax.broadcasted_iota(jnp.int32, shape, dim)


def dot(a, b):
    return jnp.dot(a, b, preferred_element_type=F32)


def kernel(n, block, lines,
           rows_hbm, order_hbm, weight_hbm, bias_hbm, table_hbm, ids_hbm,
           out_ref,
           rows, order, weight, bias, table, ids, send, recv, spread,
           local_sem, send_sem, recv_sem):
    me = lax.axis_index("tile")
    lines_dev = lines // n
    width = WD * n
    barrier = pltpu.get_barrier_semaphore()
    for k in range(1, n):
        pl.semaphore_signal(barrier, inc=1, device_id={"tile": lax.rem(me + k, n)}, device_id_type=MESH)
    loads = [
        pltpu.make_async_copy(source, target, local_sem.at[at])
        for at, (source, target) in enumerate((
            (rows_hbm, rows), (order_hbm, order), (bias_hbm, bias),
            (table_hbm, table), (ids_hbm, ids), (weight_hbm, weight)))
    ]
    for load in loads:
        load.start()

    shape = (n * block, rows.shape[0])
    at = iota(shape, 0)
    to = at >> log2(block)
    inside = at & (block - 1)
    column = (inside >> log2(lines_dev)) + to * WD - 1
    line = inside & (lines_dev - 1)
    chosen = (iota(shape, 1) == line * width + column) & (column >= 0) & (column < width) & (inside < KW * lines_dev)
    pick = jnp.where(chosen, 1.0, 0.0).astype(BF16)
    loads[0].wait()
    send[...] = dot(pick, rows[...]).astype(BF16).reshape(send.shape)

    loads[1].wait()
    received = n * block
    shape = (lines, received)
    at = iota(shape, 1)
    inside = at & (block - 1)
    position = (at >> log2(block)) * lines_dev + (inside & (lines_dev - 1))
    expand = jnp.where(iota(shape, 0) == position, 1.0, 0.0).astype(BF16)
    held = jnp.broadcast_to(order[...].astype(F32), (8, lines)).astype(BF16)
    line_of = dot(held, expand)[:1].astype(jnp.int32)
    inside = iota((1, received), 1) & (block - 1)
    slot = jnp.where(inside < KW * lines_dev, (inside >> log2(lines_dev)) * lines + line_of, -1)
    sort = jnp.where(iota((KW * lines, received), 0) == slot, 1.0, 0.0).astype(BF16)

    pl.semaphore_wait(barrier, n - 1)
    own = pltpu.make_async_copy(send.at[me], recv.at[me], local_sem.at[6])
    own.start()

    def copy_to(k):
        peer = lax.rem(me + k, n)
        return pltpu.make_async_remote_copy(
            src_ref=send.at[peer], dst_ref=recv.at[me],
            send_sem=send_sem.at[peer], recv_sem=recv_sem.at[me],
            device_id={"tile": peer}, device_id_type=MESH)

    def copy_from(k):
        peer = lax.rem(me + k, n)
        return pltpu.make_async_remote_copy(
            src_ref=send.at[peer], dst_ref=recv.at[peer],
            send_sem=send_sem.at[peer], recv_sem=recv_sem.at[peer],
            device_id={"tile": peer}, device_id_type=MESH)

    for k in range(1, n):
        copy_to(k).start()
    for load in loads[2:]:
        load.wait()

    def profile(tile):
        kind = ids[tile]
        return [jnp.full((1, 128), table[kind, c], F32) for c in range(4 * WD)]

    has_lower = jnp.where(me > 0, 1.0, 0.0)
    has_upper = jnp.where(me < n - 1, 1.0, 0.0)
    mine = profile(me)[2:-2]
    lower = [w * has_lower for w in profile(jnp.maximum(me - 1, 0))[-2:]]
    upper = [w * has_upper for w in profile(jnp.minimum(me + 1, n - 1))[:2]]
    other = lower + upper
    total = [a + b for a, b in zip(mine, other)]
    mine = [a / t for a, t in zip(mine, total)]
    other = [b / t for b, t in zip(other, total)]

    own.wait()
    for k in range(1, n):
        copy_from(k).wait_recv()
    x = dot(sort, recv[...].reshape(received, recv.shape[2])).astype(BF16)

    high = lines // LT
    channels = weight.shape[4]

    def earlier(y):
        return jnp.concatenate([y[:, :1], y[:, :-1]], axis=1)

    stage = {}
    for kh in range(3):
        taps = []
        for kw, (first, last) in enumerate(((0, 3), (1, 3), (1, 4))):
            both = jnp.concatenate([weight[kt, kh, kw] for kt in range(3)], axis=1)
            y = dot(x[first * lines:last * lines], both)
            y = y.reshape(last - first, LT, high, 3 * channels)
            y0, y1, y2 = (y[..., kt * channels:(kt + 1) * channels] for kt in range(3))
            even = earlier(y0 + y1) + y2
            odd = earlier(y0) + (y1 + y2)
            taps.append((even, odd))
        for a in range(2):
            k0, k1, k2 = (taps[kw][a] for kw in range(3))
            lower1 = k0[1] + k1[0]
            upper2 = k1[1] + k2[1]
            stage[kh, a] = (
                k0[0] + (k1[0] + k2[0]),
                lower1, lower1 + k2[1],
                upper2, upper2 + k0[1],
                (k0[2] + k1[1]) + k2[2],
            )

    zero = jnp.zeros((LT, 1, channels), F32)
    offset = bias[...].reshape(1, 1, channels)

    def act(v):
        v = v + offset
        return v / (1.0 + jnp.exp(-v))

    row_step = 2 * WD
    for a in range(2):
        for b in range(2):
            d = []
            for at in range(6):
                z0, z1, z2 = (stage[kh, a][at] for kh in range(3))
                if b == 0:
                    v = jnp.concatenate([zero, z0[:, :-1]], axis=1) + (z1 + z2)
                else:
                    v = (z0 + z1) + jnp.concatenate([z2[:, 1:], zero], axis=1)
                d.append(act(v))
            pairs = ((d[0], d[0]), (d[2], d[1]), (d[4], d[3]), (d[5], d[5]))
            for p, (own_d, other_d) in enumerate(pairs):
                value = mine[p] * own_d + other[p] * other_d
                for f in range(LT):
                    start = ((2 * f + a) * 2 * high + b) * row_step + p
                    spread[pl.ds(start, high, stride=2 * row_step), :] = value[f]
    out_ref[...] = spread[...].astype(BF16)
    for k in range(1, n):
        copy_to(k).wait_send()


def per_device(latent_rows, line_order, conv_weight, conv_bias, blend_table, blend_ids):
    n = lax.axis_size("tile")
    lines = line_order.shape[0]
    channels = latent_rows.shape[1]
    out_channels = conv_weight.shape[-1]
    lines_dev = lines // n
    block = 16 * -(-KW * lines_dev // 16)
    out_rows = 2 * lines * 2 * 2 * WD
    any_spec = pl.BlockSpec(memory_space=pl.ANY)
    out = pl.pallas_call(
        functools.partial(kernel, n, block, lines),
        out_shape=jax.ShapeDtypeStruct((out_rows, out_channels), BF16),
        in_specs=[any_spec] * 6,
        out_specs=pl.BlockSpec(memory_space=pltpu.VMEM),
        scratch_shapes=[
            pltpu.VMEM(latent_rows.shape, BF16),
            pltpu.VMEM((1, lines), jnp.int32),
            pltpu.VMEM(conv_weight.shape, BF16),
            pltpu.VMEM((1, out_channels), F32),
            pltpu.SMEM(blend_table.shape, F32),
            pltpu.SMEM(blend_ids.shape, jnp.int32),
            pltpu.VMEM((n, block, channels), BF16),
            pltpu.VMEM((n, block, channels), BF16),
            pltpu.VMEM((out_rows, out_channels), F32),
            pltpu.SemaphoreType.DMA((7,)),
            pltpu.SemaphoreType.DMA((n,)),
            pltpu.SemaphoreType.DMA((n,)),
        ],
        compiler_params=pltpu.CompilerParams(collective_id=0, has_side_effects=True),
    )(latent_rows, line_order.reshape(1, lines), conv_weight,
      conv_bias.reshape(1, out_channels), blend_table, blend_ids)
    return out.reshape(2 * LT, 2 * (lines // LT), 2 * WD, out_channels)


def solution(mesh):
    return jax.shard_map(
        per_device,
        mesh=mesh,
        in_specs=(P(("groups", "tile"), None), P("groups"), P(), P(), P(), P("groups")),
        out_specs=P("groups", None, "tile", None),
        check_vma=False,
    )
```

time: 54 us -> 13.2 us (0.24)
  matrix products: 20.3 us -> 0 us
  starting transfers between devices: 11.8 us -> 0 us
  Pallas kernels: 0 us -> 11.3 us
  local copies, waits for them, and re-layouts: 8.63 us -> 1.75 us
  waiting for transfers between devices: 6.55 us -> 0 us
  other arithmetic: 6.2 us -> 0 us
    conv_general_dilated x1 -> x0, matrix products: 20.3 us -> none  [decode_tile(): lax.conv_general_dilated(upsampled[None], conv_weight, (1, 1, 1), [(0, 0)...]
    pallas_call x0 -> x1, Pallas kernels: none -> 11.3 us  [per_device(): pl.pallas_call(functools.partial(kernel, n, block, lines), out_shape=jax....]
    all_to_all x1 -> x0, starting transfers between devices: 7.34 us -> none  [per_device(): lax.all_to_all(widened, 'tile', split_axis=1, concat_axis=0, tiled=True)]
    ppermute x2 -> x0, waiting for transfers between devices: 5.34 us -> none  [from_behind(): lax.ppermute(value, axis, [(source, source + steps) for source in range(i...]
    ppermute x2 -> x0, starting transfers between devices: 4.42 us -> none  [from_behind(): lax.ppermute(value, axis, [(source, source + steps) for source in range(i...]
    convert_element_type x3 -> x0, other arithmetic: 2.7 us -> none  [the longest x2 1.83 us: blend_profile(): (jnp.arange(blend_table.shape[0], dtype=jnp.int32) == kind_index).astype(...]
    reshape x2 -> x0, local copies, waits for them, and re-layouts: 2.47 us -> none  [the longest x1 1.47 us: upsample(): return jnp.repeat(values, 2, axis=2)]
    broadcast_in_dim x6 -> x0, local copies, waits for them, and re-layouts: 2.08 us -> none  [the longest x3 1.84 us: upsample(): return jnp.repeat(values, 2, axis=2)]
  transfers between devices with their start and end apart: 3 -> 0, of which waited for: 3 -> 0; matrix products, arithmetic and copies ran while one was open for 11% -> 0% of each run, Pallas kernels for 0% -> 0%
where the time goes in v1:
time: 13.2 us; the launch traced here: 13 us
  Pallas kernels  11.3 us (86%)
  local copies, waits for them, and re-layouts  1.75 us (13%)
    pallas_call x1, Pallas kernels, per_device(): pl.pallas_call(functools.partial(kernel, n, block, lines), out_shape=jax....  11.3 us
    unnamed x1, local copies, waits for them, and re-layouts  1.75 us

profile of v1, /device:TPU:1, one launch (start us, length us, event | category | flops | bytes accessed | tf_op | source)
XLA Modules:
  0.0 13.0 jit_solution(8922222567383737526)
XLA Ops:
  0.0 11.3 %shard_map.64 = bf16[1024,128]{1,0:T(8,128)(2,1)} custom-call(bf16[128,256]{1,0:T(8,128)(2,1)} %rows_hbm.1, s32[1,64]{1,0:T(1,128)} %bitcast.4, bf16[3,3,3,256,128]{4,3,2,1,0:T(8,128)(2,1)} %weight_hbm.1, f32[1,128]{1,0:T(1,128)} %bitcast.5, f32[4,8]{1,0:T(4,128)} %table_hbm.1, s32[16]{0:T(128)} %ids_hbm.1), custom_call_target="tpu_custom_call" | custom-call | tf_op jit(solution)/shard_map/pallas_call | solution.py:183
  11.3 1.7 %copy.8 = bf16[8,32,4,128]{3,2,1,0:T(4,128)(2,1)} copy(bf16[8,32,4,128]{3,2,1,0:T(4,128)(2,1)} %bitcast.3) | data formatting | bytes 524288

commit v2 on v1

--- a/solution.py
+++ b/solution.py
@@ -179,7 +179,7 @@
     lines_dev = lines // n
     block = 16 * -(-KW * lines_dev // 16)
     out_rows = 2 * lines * 2 * 2 * WD
-    any_spec = pl.BlockSpec(memory_space=pl.ANY)
+    any_spec = pl.BlockSpec(memory_space=pltpu.HBM)
     out = pl.pallas_call(
         functools.partial(kernel, n, block, lines),
         out_shape=jax.ShapeDtypeStruct((out_rows, out_channels), BF16),
@@ -199,9 +199,10 @@
             pltpu.SemaphoreType.DMA((n,)),
             pltpu.SemaphoreType.DMA((n,)),
         ],
-        compiler_params=pltpu.CompilerParams(collective_id=0, has_side_effects=True),
-    )(latent_rows, line_order.reshape(1, lines), conv_weight,
-      conv_bias.reshape(1, out_channels), blend_table, blend_ids)
+        compiler_params=pltpu.CompilerParams(collective_id=0, has_side_effects=True, vmem_limit_bytes=24 << 20),
+    )(*(pltpu.with_memory_space_constraint(v, pltpu.HBM) for v in (
+        latent_rows, line_order.reshape(1, lines), conv_weight,
+        conv_bias.reshape(1, out_channels), blend_table, blend_ids)))
     return out.reshape(2 * LT, 2 * (lines // LT), 2 * WD, out_channels)
 
 

time: 13.2 us -> 11.4 us (0.86)
  local copies, waits for them, and re-layouts: 1.75 us -> 0.71 us
  Pallas kernels: 11.3 us -> 10.6 us
    unnamed x1, local copies, waits for them, and re-layouts: 1.75 us -> 0.71 us
    pallas_call x1, Pallas kernels: 11.3 us -> 10.6 us  [per_device(): pl.pallas_call(functools.partial(kernel, n, block, lines), out_shape=jax....]
where the time goes in v2:
time: 11.4 us; the launch traced here: 11.3 us
  Pallas kernels  10.6 us (93%)
  local copies, waits for them, and re-layouts  0.71 us (6%)
    pallas_call x1, Pallas kernels, per_device(): pl.pallas_call(functools.partial(kernel, n, block, lines), out_shape=jax....  10.6 us
    unnamed x1, local copies, waits for them, and re-layouts  0.71 us

profile of v2, /device:TPU:1, one launch (start us, length us, event | category | flops | bytes accessed | tf_op | source)
XLA Modules:
  0.0 11.3 jit_solution(4437593266917309893)
XLA Ops:
  0.0 10.6 %shard_map.64 = bf16[1024,128]{1,0:T(8,128)(2,1)S(1)} custom-call(bf16[128,256]{1,0:T(8,128)(2,1)} %rows_hbm.1, s32[1,64]{1,0:T(1,128)} %bitcast.4, bf16[3,3,3,256,128]{4,3,2,1,0:T(8,128)(2,1)} %weight_hbm.1, f32[1,128]{1,0:T(1,128)} %bitcast.5, f32[4,8]{1,0:T(4,128)} %table_hbm.1, s32[16]{0:T(128)} %ids_hbm.1), custom_call_target="tpu_custom_call" | custom-call | tf_op jit(solution)/shard_map/pallas_call | solution.py:183
  10.6 0.7 %copy.8 = bf16[8,32,4,128]{3,2,1,0:T(4,128)(2,1)} copy(bf16[8,32,4,128]{3,2,1,0:T(4,128)(2,1)S(1)} %bitcast.3) | data formatting | bytes 524288

commit v3 on v2

--- a/solution.py
+++ b/solution.py
@@ -37,15 +37,16 @@
     lines_dev = lines // n
     width = WD * n
     barrier = pltpu.get_barrier_semaphore()
-    for k in range(1, n):
-        pl.semaphore_signal(barrier, inc=1, device_id={"tile": lax.rem(me + k, n)}, device_id_type=MESH)
     loads = [
         pltpu.make_async_copy(source, target, local_sem.at[at])
         for at, (source, target) in enumerate((
             (rows_hbm, rows), (order_hbm, order), (bias_hbm, bias),
             (table_hbm, table), (ids_hbm, ids), (weight_hbm, weight)))
     ]
-    for load in loads:
+    loads[0].start()
+    for k in range(n - 1, 0, -1):
+        pl.semaphore_signal(barrier, inc=1, device_id={"tile": lax.rem(me + k, n)}, device_id_type=MESH)
+    for load in loads[1:]:
         load.start()
 
     shape = (n * block, rows.shape[0])
@@ -59,6 +60,26 @@
     loads[0].wait()
     send[...] = dot(pick, rows[...]).astype(BF16).reshape(send.shape)
 
+    pl.semaphore_wait(barrier, n - 1)
+    own = pltpu.make_async_copy(send.at[me], recv.at[me], local_sem.at[6])
+    own.start()
+
+    def copy_to(k):
+        peer = lax.rem(me + k, n)
+        return pltpu.make_async_remote_copy(
+            src_ref=send.at[peer], dst_ref=recv.at[me],
+            send_sem=send_sem.at[peer], recv_sem=recv_sem.at[me],
+            device_id={"tile": peer}, device_id_type=MESH)
+
+    def copy_from(k):
+        peer = lax.rem(me + k, n)
+        return pltpu.make_async_remote_copy(
+            src_ref=send.at[peer], dst_ref=recv.at[peer],
+            send_sem=send_sem.at[peer], recv_sem=recv_sem.at[peer],
+            device_id={"tile": peer}, device_id_type=MESH)
+
+    for k in range(1, n):
+        copy_to(k).start()
     loads[1].wait()
     received = n * block
     shape = (lines, received)
@@ -72,26 +93,6 @@
     slot = jnp.where(inside < KW * lines_dev, (inside >> log2(lines_dev)) * lines + line_of, -1)
     sort = jnp.where(iota((KW * lines, received), 0) == slot, 1.0, 0.0).astype(BF16)
 
-    pl.semaphore_wait(barrier, n - 1)
-    own = pltpu.make_async_copy(send.at[me], recv.at[me], local_sem.at[6])
-    own.start()
-
-    def copy_to(k):
-        peer = lax.rem(me + k, n)
-        return pltpu.make_async_remote_copy(
-            src_ref=send.at[peer], dst_ref=recv.at[me],
-            send_sem=send_sem.at[peer], recv_sem=recv_sem.at[me],
-            device_id={"tile": peer}, device_id_type=MESH)
-
-    def copy_from(k):
-        peer = lax.rem(me + k, n)
-        return pltpu.make_async_remote_copy(
-            src_ref=send.at[peer], dst_ref=recv.at[peer],
-            send_sem=send_sem.at[peer], recv_sem=recv_sem.at[peer],
-            device_id={"tile": peer}, device_id_type=MESH)
-
-    for k in range(1, n):
-        copy_to(k).start()
     for load in loads[2:]:
         load.wait()
 

time: 11.4 us -> 11.2 us (0.982)
  Pallas kernels: 10.6 us -> 10.3 us
    pallas_call x1, Pallas kernels: 10.6 us -> 10.3 us  [per_device(): pl.pallas_call(functools.partial(kernel, n, block, lines), out_shape=jax....]
where the time goes in v3:
time: 11.2 us; the launch traced here: 11.1 us
  Pallas kernels  10.3 us (92%)
  local copies, waits for them, and re-layouts  0.71 us (6%)
    pallas_call x1, Pallas kernels, per_device(): pl.pallas_call(functools.partial(kernel, n, block, lines), out_shape=jax....  10.3 us
    unnamed x1, local copies, waits for them, and re-layouts  0.71 us

profile of v3, /device:TPU:1, one launch (start us, length us, event | category | flops | bytes accessed | tf_op | source)
XLA Modules:
  0.0 11.1 jit_solution(13084613939603264421)
XLA Ops:
  0.0 10.3 %shard_map.64 = bf16[1024,128]{1,0:T(8,128)(2,1)S(1)} custom-call(bf16[128,256]{1,0:T(8,128)(2,1)} %rows_hbm.1, s32[1,64]{1,0:T(1,128)} %bitcast.4, bf16[3,3,3,256,128]{4,3,2,1,0:T(8,128)(2,1)} %weight_hbm.1, f32[1,128]{1,0:T(1,128)} %bitcast.5, f32[4,8]{1,0:T(4,128)} %table_hbm.1, s32[16]{0:T(128)} %ids_hbm.1), custom_call_target="tpu_custom_call" | custom-call | tf_op jit(solution)/shard_map/pallas_call | solution.py:184
  10.4 0.7 %copy.8 = bf16[8,32,4,128]{3,2,1,0:T(4,128)(2,1)} copy(bf16[8,32,4,128]{3,2,1,0:T(4,128)(2,1)S(1)} %bitcast.3) | data formatting | bytes 524288

commit v4 on v3

--- a/solution.py
+++ b/solution.py
@@ -46,8 +46,6 @@
     loads[0].start()
     for k in range(n - 1, 0, -1):
         pl.semaphore_signal(barrier, inc=1, device_id={"tile": lax.rem(me + k, n)}, device_id_type=MESH)
-    for load in loads[1:]:
-        load.start()
 
     shape = (n * block, rows.shape[0])
     at = iota(shape, 0)
@@ -80,6 +78,8 @@
 
     for k in range(1, n):
         copy_to(k).start()
+    for load in loads[1:]:
+        load.start()
     loads[1].wait()
     received = n * block
     shape = (lines, received)

time: 11.2 us -> 11.2 us (level)
  no operation moved by 1% of the time
where the time goes in v4:
time: 11.2 us; the launch traced here: 11.1 us
  Pallas kernels  10.3 us (92%)
  local copies, waits for them, and re-layouts  0.71 us (6%)
    pallas_call x1, Pallas kernels, per_device(): pl.pallas_call(functools.partial(kernel, n, block, lines), out_shape=jax....  10.3 us
    unnamed x1, local copies, waits for them, and re-layouts  0.71 us

profile of v4, /device:TPU:1, one launch (start us, length us, event | category | flops | bytes accessed | tf_op | source)
XLA Modules:
  0.0 11.1 jit_solution(18306268361546174112)
XLA Ops:
  0.0 10.3 %shard_map.64 = bf16[1024,128]{1,0:T(8,128)(2,1)S(1)} custom-call(bf16[128,256]{1,0:T(8,128)(2,1)} %rows_hbm.1, s32[1,64]{1,0:T(1,128)} %bitcast.4, bf16[3,3,3,256,128]{4,3,2,1,0:T(8,128)(2,1)} %weight_hbm.1, f32[1,128]{1,0:T(1,128)} %bitcast.5, f32[4,8]{1,0:T(4,128)} %table_hbm.1, s32[16]{0:T(128)} %ids_hbm.1), custom_call_target="tpu_custom_call" | custom-call | tf_op jit(solution)/shard_map/pallas_call | solution.py:184
  10.4 0.7 %copy.8 = bf16[8,32,4,128]{3,2,1,0:T(4,128)(2,1)} copy(bf16[8,32,4,128]{3,2,1,0:T(4,128)(2,1)S(1)} %bitcast.3) | data formatting | bytes 524288
